TPU v7x, 128 devices: a whole 4x4x4 slice. The times are simulated.
128 devices in a mesh: pool: 4 (over y), seq: 32 (over x, z, core).
Axes of the slice: x: 4, y: 4, z: 4, core: 2. Of those that a mesh axis runs over, the one named last changes fastest.
Arguments:
- pool_kv: bfloat16 [16, 4096, 1024], P('pool', 'seq'), may hold values from -4 to 4
- span_home: int32 [12], replicated, may hold values from 0 to 15, as said below
- span_order: int32 [4, 3], P('pool'), may hold values from 0 to 11, as said below
- chosen: int32 [4, 14], P('pool'), may hold values from 0 to 95, as said below
- fresh_q: bfloat16 [4, 1792, 6144], P('pool', 'seq'), may hold values from -300 to 300
- fresh_kv: bfloat16 [4, 1792, 1024], P('pool', 'seq'), may hold values from -5 to 5
Outputs:
- attended: bfloat16 [4, 1792, 6144], P('pool', 'seq')
- decode_kv: bfloat16 [4, 32, 4, 96, 1024], P('pool', 'seq')
Inputs may be any that keep to these rules, and one draw needn't show every extreme that they name: `span_home`: all entries differ; home // 4 is the replica of a passage, and the 3 passages r * 3 to r * 3 + 2 of request r lie on different replicas; some replica holds a passage of every request. `span_order`: row r orders the passages r * 3 to r * 3 + 2. `chosen`: each row lists 14 different blocks in rising order; block k holds positions k * 128 to k * 128 + 127.
All inputs are finite; a program needn't handle non-finite values.
Results may differ from a plain program's by a relative error of at most 0.0035.
Values may be sent and summed in bfloat16 or wider, within the bound.
A program may use at most 192 MiB of HBM per device.

v0:
```python
import math
import jax
import jax.numpy as jnp
from jax import lax
from jax.sharding import PartitionSpec as P

KV_HEADS = 4
HEAD_DIM = 128
masked_low = -1e30


def patch_rows(values, positions, picked, fresh_all, block_len):
    block_ids = positions // block_len
    offsets = positions % block_len
    matches = block_ids[..., None] == picked
    is_fresh = jnp.any(matches, axis=-1)
    slot_ids = jnp.sum(jnp.where(matches, jnp.arange(picked.shape[0], dtype=jnp.int32), 0), axis=-1)
    source = (slot_ids * block_len + offsets).reshape(-1)
    rows_new = jnp.take(fresh_all, source, axis=0).reshape(values.shape)
    return jnp.where(is_fresh[..., None], rows_new, values)


def fold_keys(state_in, shard_piece, queries, query_pos, span_len):
    span_count, piece_rows, kv_width = shard_piece.shape
    key_pos = (
        jnp.arange(span_count, dtype=jnp.int32)[:, None] * span_len
        + jnp.arange(piece_rows, dtype=jnp.int32)[None, :]
    )
    kv_heads, query_rows, head_dim = queries.shape
    flattened = shard_piece.reshape(span_count * piece_rows, kv_heads, 2, head_dim)
    keys_all = flattened[:, :, 0]
    values_all = flattened[:, :, 1]
    pos_all = key_pos.reshape(-1)
    key_count = span_count * piece_rows
    step_len = math.gcd(key_count, 512)
    inv_root = head_dim ** (-0.5)

    def one_block(state_now, turn_at):
        running_max, total_weight, weighted = state_now
        first_key = turn_at * step_len
        key_blk = lax.dynamic_slice_in_dim(keys_all, first_key, step_len, 0)
        value_blk = lax.dynamic_slice_in_dim(values_all, first_key, step_len, 0)
        pos_blk = lax.dynamic_slice_in_dim(pos_all, first_key, step_len, 0)
        scores = (
            jnp.einsum("hqd,khd->hqk", queries, key_blk, preferred_element_type=jnp.float32)
            * inv_root
        )
        allowed = pos_blk[None, None, :] <= query_pos[None, :, None]
        scores = jnp.where(allowed, scores, masked_low)
        newest = jnp.maximum(running_max, jnp.max(scores, axis=-1))
        weights = jnp.where(allowed, jnp.exp(scores - newest[..., None]), 0.0)
        factor = jnp.exp(running_max - newest)
        total_weight = total_weight * factor + jnp.sum(weights, axis=-1)
        weighted = weighted * factor[..., None] + jnp.einsum(
            "hqk,khd->hqd",
            weights.astype(jnp.bfloat16),
            value_blk,
            preferred_element_type=jnp.float32,
        )
        return ((newest, total_weight, weighted), None)

    state_out, _ = lax.scan(one_block, state_in, jnp.arange(key_count // step_len))
    return state_out


def shards(pool_kv, span_home, span_order, chosen, fresh_q, fresh_kv):
    pool_count = lax.axis_size("pool")
    seq_count = lax.axis_size("seq")
    replica = lax.axis_index("pool")
    my_seat = lax.axis_index("seq")
    slot_count, block_len, kv_width = pool_kv.shape
    span_count = span_order.shape[1]
    span_len = block_len * seq_count
    head_dim = HEAD_DIM
    kv_heads = KV_HEADS
    picked = chosen[0]
    span_total = span_home.shape[0]
    home_replica = span_home // slot_count
    home_slot = span_home % slot_count
    span_request = jnp.arange(span_total, dtype=jnp.int32) // span_count
    requests = jnp.arange(pool_count, dtype=jnp.int32)
    held = (home_replica == replica)[None, :] & (span_request[None, :] == requests[:, None])
    in_slot = home_slot[None, :, None] == jnp.arange(slot_count, dtype=jnp.int32)[None, None, :]
    selector = jnp.any(held[:, :, None] & in_slot, axis=1).astype(jnp.bfloat16)
    outgoing = jnp.einsum(
        "rk,ktc->rtc", selector, pool_kv, preferred_element_type=jnp.float32
    ).astype(jnp.bfloat16)
    arrived = lax.all_to_all(outgoing, "pool", split_axis=0, concat_axis=0, tiled=True)
    order_row = span_order[0]
    lookup = order_row[:, None] == jnp.arange(span_total, dtype=jnp.int32)[None, :]
    source_replica = jnp.sum(jnp.where(lookup, home_replica[None, :], 0), axis=1)
    chooser = (source_replica[:, None] == requests[None, :]).astype(jnp.bfloat16)
    cached = jnp.einsum("jp,ptc->jtc", chooser, arrived, preferred_element_type=jnp.float32).astype(
        jnp.bfloat16
    )
    fresh_all = lax.all_gather(fresh_kv[0], "seq", axis=0, tiled=True)
    block_ids = jnp.arange(span_count, dtype=jnp.int32)[:, None] * seq_count + my_seat
    local_pos = block_ids * block_len + jnp.arange(block_len, dtype=jnp.int32)[None, :]
    patched = patch_rows(cached, local_pos, picked, fresh_all, block_len)
    row_count = fresh_q.shape[1]
    q_width = fresh_q.shape[2]
    group = q_width // (kv_heads * head_dim)
    list_rows = my_seat * row_count + jnp.arange(row_count, dtype=jnp.int32)
    list_block = list_rows // block_len
    base_block = jnp.sum(
        jnp.where(
            list_block[:, None] == jnp.arange(picked.shape[0], dtype=jnp.int32)[None, :],
            picked[None, :],
            0,
        ),
        axis=1,
    )
    query_pos = base_block * block_len + list_rows % block_len
    queries = fresh_q[0].reshape(row_count, kv_heads, group, head_dim).transpose(1, 2, 0, 3)
    queries = queries.reshape(kv_heads, group * row_count, head_dim)
    pos_tiled = jnp.tile(query_pos, group)
    start_state = (
        jnp.full((kv_heads, group * row_count), masked_low, jnp.float32),
        jnp.zeros((kv_heads, group * row_count), jnp.float32),
        jnp.zeros((kv_heads, group * row_count, head_dim), jnp.float32),
    )
    final_state = fold_keys(
        start_state,
        lax.all_gather(patched, "seq", axis=1, tiled=True),
        queries,
        pos_tiled,
        span_len,
    )
    running_max, total_weight, weighted = final_state
    attended = (weighted / total_weight[..., None]).reshape(kv_heads, group, row_count, head_dim)
    attended = attended.transpose(2, 0, 1, 3).reshape(1, row_count, q_width).astype(jnp.bfloat16)
    per_group = kv_heads // pool_count
    run_len = block_len // seq_count
    laid = patched.reshape(span_count, seq_count, run_len, pool_count, per_group, 2 * head_dim)
    laid = laid.transpose(3, 1, 4, 0, 2, 5).reshape(
        pool_count, seq_count, per_group, span_count, run_len * 2 * head_dim
    )
    merged = laid.reshape(pool_count * seq_count, per_group, span_count, run_len * 2 * head_dim)
    landed = lax.all_to_all(merged, ("pool", "seq"), split_axis=0, concat_axis=0, tiled=True)
    landed = landed.reshape(pool_count, seq_count, per_group, span_count, run_len * 2 * head_dim)
    decoded = landed.transpose(2, 0, 3, 1, 4).reshape(
        per_group, 1, pool_count, span_count * seq_count, run_len * 2 * head_dim
    )
    return (attended, decoded)


def solution(mesh):
    in_specs = (
        P("pool", "seq", None),
        P(),
        P("pool", None),
        P("pool", None),
        P("pool", "seq", None),
        P("pool", "seq", None),
    )
    out_specs = (P("pool", "seq", None), P("pool", "seq", None, None, None))
    return jax.shard_map(shards, mesh=mesh, in_specs=in_specs, out_specs=out_specs, check_vma=False)
```

profile of v0, /device:TPU:1, one launch (start us, length us, event | category | flops | bytes accessed | tf_op | source)
XLA Modules:
  0.0 632.1 jit_solution(8040437564425881074)
XLA Ops:
  11.7 5.0 all-to-all-start
  17.5 42.0 %all-gather.6.cloned.1.call-done = bf16[1,1792,1024]{2,1,0:T(8,128)(2,1)} async-done(((bf16[1,56,1024]{2,1,0:T(8,128)(2,1)}), bf16[1,1792,1024]{2,1,0:T(8,128)(2,1)}) %all-gather.6.cloned.1.call-update) | async-done | bytes 3670032 | tf_op jit(solution)/shard_map/all_gather | solution.py:96
  59.5 5.3 gather_fusion
  71.5 7.2 %all-to-all-start.1 = ((bf16[128,1,3,1024]{3,2,1,0:T(4,128)(2,1)}), bf16[128,1,3,1024]{3,2,1,0:T(4,128)(2,1)S(1)}, u32[]{:S(2)}, u32[]{:S(2)}) async-start(bf16[128,1,3,1024]{3,2,1,0:T(4,128)(2,1)} %reshape.349), calls=%async_computation.1 | async-start | bytes 2097152 | tf_op jit(solution)/shard_map/all_to_all | solution.py:139
  81.1 27.9 %all-to-all-done.1 = bf16[128,1,3,1024]{3,2,1,0:T(4,128)(2,1)S(1)} async-done(((bf16[128,1,3,1024]{3,2,1,0:T(4,128)(2,1)}), bf16[128,1,3,1024]{3,2,1,0:T(4,128)(2,1)S(1)}, u32[]{:S(2)}, u32[]{:S(2)}) %all-to-all-start.1) | async-done | bytes 786464 | tf_op jit(solution)/shard_map/all_to_all | solution.py:139
  110.2 60.9 %all-gather.4.cloned.1.call-done = bf16[3,4096,1024]{2,1,0:T(8,128)(2,1)} async-done(((bf16[3,128,1024]{2,1,0:T(8,128)(2,1)}), bf16[3,4096,1024]{2,1,0:T(8,128)(2,1)}) %all-gather.4.cloned.1.call-update) | async-done | bytes 25165840 | tf_op jit(solution)/shard_map/all_gather | solution.py:124
  171.1 40.5 %reshape.332 = bf16[12288,4,2,128]{3,2,1,0:T(2,128)(2,1)} reshape(bf16[3,4096,1024]{2,1,0:T(8,128)(2,1)} %all-gather.4.cloned.1.call-done) | data formatting | bytes 50331648 | tf_op jit(solution)/shard_map/reshape | solution.py:30
  211.6 47.1 %fusion.38 = (bf16[12288,4,1,128]{3,2,1,0:T(2,128)(2,1)}, bf16[12288,4,1,128]{3,2,1,0:T(2,128)(2,1)}) fusion(bf16[12288,4,2,128]{3,2,1,0:T(2,128)(2,1)} %reshape.332), kind=kLoop, calls=%fused_computation.93 | loop fusion | bytes 50331648 | tf_op jit(solution)/shard_map/slice | solution.py:32
  258.7 27.3 %copy_bitcast_fusion = (bf16[12288,4,128]{2,0,1:T(8,128)(2,1)}, bf16[12288,4,128]{2,0,1:T(8,128)(2,1)}) fusion(bf16[12288,4,1,128]{3,2,1,0:T(2,128)(2,1)} %get-tuple-element.129, bf16[12288,4,1,128]{3,2,1,0:T(2,128)(2,1)} %get-tuple-element.130), kind=kLoop, calls=%fused_computation.24 | loop fusion | bytes 50331648 | tf_op jit(solution)/shard_map/squeeze | solution.py:32
  286.1 337.2 %while.15 = (s32[]{:T(128)}, f32[4,672]{1,0:T(4,128)S(1)}, f32[4,672]{1,0:T(4,128)S(1)}, f32[4,672,128]{2,1,0:T(8,128)S(1)}, s32[24]{0:T(128)S(1)}, /*index=5*/s...) while((s32[]{:T(128)}, f32[4,672]{1,0:T(4,128)S(1)}, ...), condition=%wide.region_8.9_spmd.clone, body=%wide.region_5.8_spmd.clone.sunk | while | flops 723924096 | bytes 44590032 | solution.py:62
  287.9 4.5 fusion.50
  292.4 4.4 fusion.51
  301.9 4.5 fusion.50
  306.4 4.4 fusion.51
  310.9 3.3 fusion.53
  316.0 4.5 fusion.50
  320.5 4.4 fusion.51
  330.0 4.5 fusion.50
  334.5 4.4 fusion.51
  344.1 4.5 fusion.50
  348.6 4.4 fusion.51
  353.0 3.3 fusion.53
  358.1 4.5 fusion.50
  362.6 4.4 fusion.51
  372.2 4.5 fusion.50
  376.7 4.4 fusion.51
  386.2 4.5 fusion.50
  390.7 4.4 fusion.51
  400.3 4.5 fusion.50
  404.8 4.4 fusion.51
  414.3 4.5 fusion.50
  418.8 4.4 fusion.51
  428.4 4.5 fusion.50
  432.9 4.4 fusion.51
  437.3 3.3 fusion.53
  442.4 4.5 fusion.50
  446.9 4.4 fusion.51
  456.5 4.5 fusion.50
  461.0 4.4 fusion.51
  470.5 4.5 fusion.50
  475.0 4.4 fusion.51
  484.6 4.5 fusion.50
  489.1 4.4 fusion.51
  498.6 4.5 fusion.50
  503.1 4.4 fusion.51
  512.7 4.5 fusion.50
  517.2 4.4 fusion.51
  521.6 3.3 fusion.53
  526.7 4.5 fusion.50
  531.2 4.4 fusion.51
  540.8 4.5 fusion.50
  545.3 4.4 fusion.51
  554.8 4.5 fusion.50
  559.3 4.4 fusion.51
  563.7 3.3 fusion.53
  568.9 4.5 fusion.50
  573.4 4.4 fusion.51
  582.9 4.5 fusion.50
  587.4 4.4 fusion.51
  597.0 4.5 fusion.50
  601.5 4.4 fusion.51
  605.9 3.3 fusion.53
  611.0 4.5 fusion.50
  615.5 4.4 fusion.51
  (315 shorter events, 103.6 us)
Async XLA Ops:
  7.2 2.3 copy-start
  7.2 9.6 %copy-start.4 = (s32[1,14]{1,0:T(1,128)S(1)}, s32[1,14]{1,0:T(1,128)}, u32[]{:S(2)}) copy-start(s32[1,14]{1,0:T(1,128)} %param.11) | copy-start | bytes 172
  7.2 10.2 %copy-start.5 = (s32[1,3]{1,0:T(1,128)S(1)}, s32[1,3]{1,0:T(1,128)}, u32[]{:S(2)}) copy-start(s32[1,3]{1,0:T(1,128)} %param.10) | copy-start | bytes 40
  7.2 52.3 %all-gather.6.cloned.1.call-start = ((), (), s32[]{:S(2)}) async-start(), calls=%async_computation.3 | async-start | bytes 3784704 | tf_op jit(solution)/shard_map/all_gather | solution.py:96
  11.7 53.2 %all-to-all-start = ((bf16[4,128,1024]{2,1,0:T(8,128)(2,1)}), bf16[4,128,1024]{2,1,0:T(8,128)(2,1)S(1)}, u32[]{:S(2)}, u32[]{:S(2)}) async-start(bf16[4,128,1024]{2,1,0:T(8,128)(2,1)} %copy.49), calls=%async_computation | async-start | bytes 2097152 | tf_op jit(solution)/shard_map/all_to_all | solution.py:88
  16.6 154.5 %all-gather.4.cloned.1.call-start = ((), (), s32[]{:S(2)}) async-start(), calls=%async_computation.2 | async-start | bytes 25952256 | tf_op jit(solution)/shard_map/all_gather | solution.py:124
  71.5 37.4 %all-to-all-start.1 = ((bf16[128,1,3,1024]{3,2,1,0:T(4,128)(2,1)}), bf16[128,1,3,1024]{3,2,1,0:T(4,128)(2,1)S(1)}, u32[]{:S(2)}, u32[]{:S(2)}) async-start(bf16[128,1,3,1024]{3,2,1,0:T(4,128)(2,1)} %reshape.349), calls=%async_computation.1 | async-start | bytes 2097152 | tf_op jit(solution)/shard_map/all_to_all | solution.py:139
  258.7 27.3 %copy-start.3 = (f32[4,672,128]{2,1,0:T(8,128)S(1)}, f32[4,672,128]{2,1,0:T(8,128)}, u32[]{:S(2)}) copy-start(f32[4,672,128]{2,1,0:T(8,128)} %custom-call.2) | copy-start | bytes 4128772
  292.4 4.4 copy-start.2
  306.4 4.4 copy-start.2
  320.5 4.4 copy-start.2
  334.5 4.4 copy-start.2
  348.6 4.4 copy-start.2
  362.6 4.4 copy-start.2
  376.7 4.4 copy-start.2
  390.7 4.4 copy-start.2
  404.8 4.4 copy-start.2
  418.8 4.4 copy-start.2
  432.9 4.4 copy-start.2
  446.9 4.4 copy-start.2
  461.0 4.4 copy-start.2
  475.0 4.4 copy-start.2
  489.1 4.4 copy-start.2
  503.1 4.4 copy-start.2
  517.2 4.4 copy-start.2
  531.2 4.4 copy-start.2
  545.3 4.4 copy-start.2
  559.3 4.4 copy-start.2
  573.4 4.4 copy-start.2
  587.4 4.4 copy-start.2
  601.5 4.4 copy-start.2
  615.5 4.4 copy-start.2
  623.3 2.0 copy-start.1
Sparse Core Ops, SparseCore 0:
  10.3 49.2 all-gather.5
  69.1 102.0 all-gather.3
where the time goes:
time: 636 us; the launch traced here: 632 us
  matrix products  191 us (30%)
  local copies, waits for them, and re-layouts  150 us (24%)
  waiting for transfers between devices  131 us (21%)
  other arithmetic  114 us (18%)
  loops' own time  18.3 us (3%)
  between operations  14.3 us (2%)
  starting transfers between devices  12.2 us (2%)
    dot_general x24, matrix products, one_block(): jnp.einsum('hqd,khd->hqk', queries, key_blk, preferred_element_type=jnp.f...  108 us
    reduce_sum x24, other arithmetic, one_block(): total_weight = total_weight * factor + jnp.sum(weights, axis=-1)  105 us
    dot_general x24, matrix products, one_block(): jnp.einsum('hqk,khd->hqd', weights.astype(jnp.bfloat16), value_blk, prefe...  79.2 us
    all_gather x1, waiting for transfers between devices, shards(): lax.all_gather(patched, 'seq', axis=1, tiled=True)  60.9 us
    slice x1, local copies, waits for them, and re-layouts, fold_keys(): values_all = flattened[:, :, 1]  47.1 us
    all_gather x1, waiting for transfers between devices, shards(): fresh_all = lax.all_gather(fresh_kv[0], 'seq', axis=0, tiled=True)  42 us
    reshape x1, local copies, waits for them, and re-layouts, fold_keys(): shard_piece.reshape(span_count * piece_rows, kv_heads, 2, head_dim)  40.5 us
    all_to_all x1, waiting for transfers between devices, shards(): lax.all_to_all(merged, ('pool', 'seq'), split_axis=0, concat_axis=0, tile...  27.9 us
  transfers between devices with their start and end apart: 4, of which 3 were waited for; matrix products, arithmetic and copies ran while one was open for 3% of the time, Pallas kernels for 0%

commit v1 on v0

--- a/solution.py
+++ b/solution.py
@@ -1,3 +1,4 @@
+import functools
 import math
 import jax
 import jax.numpy as jnp
@@ -7,6 +8,13 @@
 KV_HEADS = 4
 HEAD_DIM = 128
 masked_low = -1e30
+
+
+def return_all_pools_up(xin, k_dim):
+    return jnp.concatenate(lax.all_gather(xin, axis_name="seq"), axis=k_dim)
+
+
+get_the_panels = functools.partial(return_all_pools_up, k_dim=1)
 
 
 def patch_rows(values, positions, picked, fresh_all, block_len):
@@ -119,13 +127,7 @@
         jnp.zeros((kv_heads, group * row_count), jnp.float32),
         jnp.zeros((kv_heads, group * row_count, head_dim), jnp.float32),
     )
-    final_state = fold_keys(
-        start_state,
-        lax.all_gather(patched, "seq", axis=1, tiled=True),
-        queries,
-        pos_tiled,
-        span_len,
-    )
+    final_state = fold_keys(start_state, get_the_panels(patched), queries, pos_tiled, span_len)
     running_max, total_weight, weighted = final_state
     attended = (weighted / total_weight[..., None]).reshape(kv_heads, group, row_count, head_dim)
     attended = attended.transpose(2, 0, 1, 3).reshape(1, row_count, q_width).astype(jnp.bfloat16)

time: 636 us -> 608 us (0.956)
  local copies, waits for them, and re-layouts: 150 us -> 121 us
    slice x1 -> x0, local copies, waits for them, and re-layouts: 47.1 us -> none  [fold_keys(): values_all = flattened[:, :, 1]]
    another operation x0 -> x1, local copies, waits for them, and re-layouts: none -> 35.5 us  [fold_keys(): shard_piece.reshape(span_count * piece_rows, kv_heads, 2, head_dim)]
    squeeze x1, local copies, waits for them, and re-layouts: 27.3 us -> 17.8 us  [fold_keys(): values_all = flattened[:, :, 1]]
    reshape x1, local copies, waits for them, and re-layouts: 40.5 us -> 32 us  [return_all_pools_up(): return jnp.concatenate(lax.all_gather(xin, axis_name='seq'), axis=k_dim)]
where the time goes in v1:
time: 608 us; the launch traced here: 604 us
  matrix products  192 us (32%)
  waiting for transfers between devices  131 us (22%)
  local copies, waits for them, and re-layouts  121 us (20%)
  other arithmetic  114 us (19%)
  loops' own time  18.3 us (3%)
  between operations  14.3 us (2%)
  starting transfers between devices  12.2 us (2%)
    dot_general x24, matrix products, one_block(): jnp.einsum('hqd,khd->hqk', queries, key_blk, preferred_element_type=jnp.f...  108 us
    reduce_sum x24, other arithmetic, one_block(): total_weight = total_weight * factor + jnp.sum(weights, axis=-1)  105 us
    dot_general x24, matrix products, one_block(): jnp.einsum('hqk,khd->hqd', weights.astype(jnp.bfloat16), value_blk, prefe...  80.7 us
    all_gather x1, waiting for transfers between devices, return_all_pools_up(): return jnp.concatenate(lax.all_gather(xin, axis_name='seq'), axis=k_dim)  60.9 us
    all_gather x1, waiting for transfers between devices, shards(): fresh_all = lax.all_gather(fresh_kv[0], 'seq', axis=0, tiled=True)  42 us
    another operation x1, local copies, waits for them, and re-layouts, fold_keys(): shard_piece.reshape(span_count * piece_rows, kv_heads, 2, head_dim)  35.5 us
    reshape x1, local copies, waits for them, and re-layouts, return_all_pools_up(): return jnp.concatenate(lax.all_gather(xin, axis_name='seq'), axis=k_dim)  32 us
    all_to_all x1, waiting for transfers between devices, shards(): lax.all_to_all(merged, ('pool', 'seq'), split_axis=0, concat_axis=0, tile...  27.9 us
  transfers between devices with their start and end apart: 4, of which 3 were waited for; matrix products, arithmetic and copies ran while one was open for 3% of the time, Pallas kernels for 0%

profile of v1, /device:TPU:1, one launch (start us, length us, event | category | flops | bytes accessed | tf_op | source)
XLA Modules:
  0.0 603.7 jit_solution(9825637824606594888)
XLA Ops:
  11.7 5.0 all-to-all-start
  17.5 42.0 %all-gather.5.cloned.1.call-done = bf16[1,1792,1024]{2,1,0:T(8,128)(2,1)} async-done(((bf16[1,56,1024]{2,1,0:T(8,128)(2,1)}), bf16[1,1792,1024]{2,1,0:T(8,128)(2,1)}) %all-gather.5.cloned.1.call-update) | async-done | bytes 3670032 | tf_op jit(solution)/shard_map/all_gather | solution.py:104
  59.5 5.3 gather_fusion
  71.5 7.2 %all-to-all-start.1 = ((bf16[128,1,3,1024]{3,2,1,0:T(4,128)(2,1)}), bf16[128,1,3,1024]{3,2,1,0:T(4,128)(2,1)S(1)}, u32[]{:S(2)}, u32[]{:S(2)}) async-start(bf16[128,1,3,1024]{3,2,1,0:T(4,128)(2,1)} %reshape.350), calls=%async_computation.1 | async-start | bytes 2097152 | tf_op jit(solution)/shard_map/all_to_all | solution.py:141
  81.1 27.9 %all-to-all-done.1 = bf16[128,1,3,1024]{3,2,1,0:T(4,128)(2,1)S(1)} async-done(((bf16[128,1,3,1024]{3,2,1,0:T(4,128)(2,1)}), bf16[128,1,3,1024]{3,2,1,0:T(4,128)(2,1)S(1)}, u32[]{:S(2)}, u32[]{:S(2)}) %all-to-all-start.1) | async-done | bytes 786464 | tf_op jit(solution)/shard_map/all_to_all | solution.py:141
  110.2 60.9 %all-gather.7.cloned.1.call-done = bf16[96,128,1024]{2,1,0:T(8,128)(2,1)} async-done(((bf16[3,128,1024]{2,1,0:T(8,128)(2,1)}), bf16[96,128,1024]{2,1,0:T(8,128)(2,1)}) %all-gather.7.cloned.1.call-update) | async-done | bytes 25165840 | tf_op jit(solution)/shard_map/all_gather | solution.py:14
  171.1 32.0 %copy.55 = bf16[3,32,128,1024]{2,1,0,3:T(8,128)(2,1)} copy(bf16[3,32,128,1024]{3,2,0,1:T(8,128)(2,1)} %bitcast.79) | data formatting | bytes 50331648 | tf_op jit(solution)/shard_map/reshape | solution.py:14
  203.1 35.5 %reshape_reshape.6 = bf16[12288,4,2,128]{0,3,2,1:T(8,128)(2,1)} reshape(bf16[3,32,128,1024]{2,1,0,3:T(8,128)(2,1)} %copy.55) | data formatting | bytes 50331648 | tf_op jit(solution)/shard_map/reshape;reshape | solution.py:38
  238.6 17.8 %slice_bitcast_fusion = (bf16[12288,4,128]{0,2,1:T(8,128)(2,1)}, bf16[12288,4,128]{0,2,1:T(8,128)(2,1)}) fusion(bf16[12288,4,2,128]{0,3,2,1:T(8,128)(2,1)} %reshape_reshape.6), kind=kLoop, calls=%fused_computation.24 | loop fusion | bytes 50331648 | tf_op jit(solution)/shard_map/squeeze | solution.py:40
  256.5 338.3 %while.15 = (s32[]{:T(128)}, f32[4,672]{1,0:T(4,128)S(1)}, f32[4,672]{1,0:T(4,128)S(1)}, f32[4,672,128]{2,1,0:T(8,128)S(1)}, s32[24]{0:T(128)S(1)}, /*index=5*/s...) while((s32[]{:T(128)}, f32[4,672]{1,0:T(4,128)S(1)}, ...), condition=%wide.region_8.9_spmd.clone, body=%wide.region_5.8_spmd.clone.sunk | while | flops 723924096 | bytes 44590032 | solution.py:70
  258.3 4.5 fusion.49
  262.8 4.4 fusion.50
  267.2 3.4 fusion.52
  272.4 4.5 fusion.49
  276.9 4.4 fusion.50
  286.5 4.5 fusion.49
  291.0 4.4 fusion.50
  295.4 3.4 fusion.52
  300.6 4.5 fusion.49
  305.1 4.4 fusion.50
  314.7 4.5 fusion.49
  319.2 4.4 fusion.50
  323.6 3.4 fusion.52
  328.8 4.5 fusion.49
  333.3 4.4 fusion.50
  342.9 4.5 fusion.49
  347.4 4.4 fusion.50
  351.8 3.4 fusion.52
  357.0 4.5 fusion.49
  361.5 4.4 fusion.50
  371.1 4.5 fusion.49
  375.6 4.4 fusion.50
  380.0 3.4 fusion.52
  385.2 4.5 fusion.49
  389.7 4.4 fusion.50
  399.3 4.5 fusion.49
  403.8 4.4 fusion.50
  408.2 3.4 fusion.52
  413.4 4.5 fusion.49
  417.9 4.4 fusion.50
  427.5 4.5 fusion.49
  432.0 4.4 fusion.50
  441.6 4.5 fusion.49
  446.1 4.4 fusion.50
  455.7 4.5 fusion.49
  460.2 4.4 fusion.50
  469.8 4.5 fusion.49
  474.3 4.4 fusion.50
  483.9 4.5 fusion.49
  488.4 4.4 fusion.50
  498.0 4.5 fusion.49
  502.5 4.4 fusion.50
  512.1 4.5 fusion.49
  516.6 4.4 fusion.50
  526.2 4.5 fusion.49
  530.7 4.4 fusion.50
  540.3 4.5 fusion.49
  544.7 4.4 fusion.50
  554.3 4.5 fusion.49
  558.8 4.4 fusion.50
  568.4 4.5 fusion.49
  572.9 4.4 fusion.50
  582.5 4.5 fusion.49
  587.0 4.4 fusion.50
  (315 shorter events, 104.8 us)
Async XLA Ops:
  7.2 2.3 copy-start
  7.2 9.6 %copy-start.4 = (s32[1,14]{1,0:T(1,128)S(1)}, s32[1,14]{1,0:T(1,128)}, u32[]{:S(2)}) copy-start(s32[1,14]{1,0:T(1,128)} %param.11) | copy-start | bytes 172
  7.2 10.2 %copy-start.5 = (s32[1,3]{1,0:T(1,128)S(1)}, s32[1,3]{1,0:T(1,128)}, u32[]{:S(2)}) copy-start(s32[1,3]{1,0:T(1,128)} %param.10) | copy-start | bytes 40
  7.2 52.3 %all-gather.5.cloned.1.call-start = ((), (), s32[]{:S(2)}) async-start(), calls=%async_computation.2 | async-start | bytes 3784704 | tf_op jit(solution)/shard_map/all_gather | solution.py:104
  11.7 53.2 %all-to-all-start = ((bf16[4,128,1024]{2,1,0:T(8,128)(2,1)}), bf16[4,128,1024]{2,1,0:T(8,128)(2,1)S(1)}, u32[]{:S(2)}, u32[]{:S(2)}) async-start(bf16[4,128,1024]{2,1,0:T(8,128)(2,1)} %copy.52), calls=%async_computation | async-start | bytes 2097152 | tf_op jit(solution)/shard_map/all_to_all | solution.py:96
  16.6 154.5 %all-gather.7.cloned.1.call-start = ((), (), s32[]{:S(2)}) async-start(), calls=%async_computation.3 | async-start | bytes 25952256 | tf_op jit(solution)/shard_map/all_gather | solution.py:14
  71.5 37.4 %all-to-all-start.1 = ((bf16[128,1,3,1024]{3,2,1,0:T(4,128)(2,1)}), bf16[128,1,3,1024]{3,2,1,0:T(4,128)(2,1)S(1)}, u32[]{:S(2)}, u32[]{:S(2)}) async-start(bf16[128,1,3,1024]{3,2,1,0:T(4,128)(2,1)} %reshape.350), calls=%async_computation.1 | async-start | bytes 2097152 | tf_op jit(solution)/shard_map/all_to_all | solution.py:141
  238.6 17.9 %copy-start.3 = (f32[4,672,128]{2,1,0:T(8,128)S(1)}, f32[4,672,128]{2,1,0:T(8,128)}, u32[]{:S(2)}) copy-start(f32[4,672,128]{2,1,0:T(8,128)} %custom-call.2) | copy-start | bytes 4128772
  262.8 4.4 copy-start.2
  276.9 4.4 copy-start.2
  291.0 4.4 copy-start.2
  305.1 4.4 copy-start.2
  319.2 4.4 copy-start.2
  333.3 4.4 copy-start.2
  347.4 4.4 copy-start.2
  361.5 4.4 copy-start.2
  375.6 4.4 copy-start.2
  389.7 4.4 copy-start.2
  403.8 4.4 copy-start.2
  417.9 4.4 copy-start.2
  432.0 4.4 copy-start.2
  446.1 4.4 copy-start.2
  460.2 4.4 copy-start.2
  474.3 4.4 copy-start.2
  488.4 4.4 copy-start.2
  502.5 4.4 copy-start.2
  516.5 4.4 copy-start.2
  530.6 4.4 copy-start.2
  544.7 4.4 copy-start.2
  558.8 4.4 copy-start.2
  572.9 4.4 copy-start.2
  587.0 4.4 copy-start.2
  594.8 2.0 copy-start.1
Sparse Core Ops, SparseCore 0:
  10.3 49.2 all-gather.4
  69.1 102.0 all-gather.6
